TPU v7x, 256 devices: a whole 4x4x8 slice. The times are simulated.
256 devices in a mesh: circ: 64 (over x_lo, y, z), span: 4 (over x_hi, core).
Axes of the slice: x: 4 (x_hi: 2, x_lo: 2; x = x_hi * 2 + x_lo), y: 4, z: 8, core: 2. Of those that a mesh axis runs over, the one named last changes fastest.
Arguments:
- coefficients: float32 [65, 5, 16, 4096], P(None, None, 'span', 'circ'), may hold values from -3 to 3
- local_step: float32 [16, 2048, 256], P('span', 'circ'), may hold values from 0.1 to 0.4
- jacobian: float32 [3, 5, 5], replicated, may hold values from -2.5 to 2.5
- harmonic_numbers: int32 [32], replicated, may hold values from 1 to 64
- nodal_diameter: int32 [1], replicated, may hold values from 1 to 64
Outputs:
- new_state: float32 [5, 16, 2048, 256], P(None, 'span', 'circ')
All inputs are finite; a program needn't handle non-finite values.
Results may differ from a plain program's by a relative error of at most 0.0001.
Values sent between devices are 32-bit elements; how exact they have to be, the bound alone decides.
No kernel may reach another device: no remote copies, remote signals or barrier semaphores. Data moves between devices by JAX's collectives and lax.ppermute only.
A program may use at most 128 MiB of HBM per device.

v0:
```python
import math
import jax
import jax.numpy as jnp
from jax import lax
from jax.sharding import PartitionSpec as P

VARS = 5
PASS_DEV = 2
PITCH = 16
AXIAL = 256
section_weight = 0.5
dissipation = 0.125


def extended(array, sides, width, wrap):
    for axis, dim in sides:
        count, length = (lax.axis_size(axis), array.shape[dim])
        up = [(i, (i + 1) % count) for i in range(count if wrap else count - 1)]
        down = [(j, i) for i, j in up]
        last = lax.slice_in_dim(array, length - width, length, axis=dim)
        initial = lax.slice_in_dim(array, 0, width, axis=dim)
        before = lax.ppermute(last, axis, up)
        after = lax.ppermute(initial, axis, down)
        array = jnp.concatenate([before, array, after], axis=dim)
    return array


def phase_table(harmonic_numbers, nodal_diameter, passages, cycle_count):
    phase_turn = harmonic_numbers[None, :] * nodal_diameter[0] % cycle_count
    phase_turn = phase_turn * passages[:, None] % cycle_count
    phase_angle = phase_turn.astype(jnp.float32) * jnp.float32(2.0 * math.pi / cycle_count)
    mean_column = jnp.ones((passages.shape[0], 1), jnp.float32)
    return jnp.concatenate([mean_column, jnp.cos(phase_angle), jnp.sin(phase_angle)], axis=1)


def section_update(flow_state, span_pad, pitch_pad, jacobian, local_step):
    axial_pad = jnp.pad(flow_state, ((0, 0), (0, 0), (0, 0), (1, 1)))
    neighbours = [
        (span_pad[:, 2:], span_pad[:, :-2]),
        (pitch_pad[:, :, 2:], pitch_pad[:, :, :-2]),
        (axial_pad[:, :, :, 2:], axial_pad[:, :, :, :-2]),
    ]
    resid = jnp.zeros(flow_state.shape, jnp.float32)
    for direction in range(3):
        plus_side, minus_side = neighbours[direction]
        flux_part = jnp.einsum(
            "vw,wsqa->vsqa",
            jacobian[direction],
            0.5 * (plus_side - minus_side),
            precision=lax.Precision.HIGHEST,
        )
        resid = resid + flux_part - dissipation * (plus_side - 2.0 * flow_state + minus_side)
    return flow_state - section_weight * local_step[None] * resid


def send_rims(flow_state):
    return extended(flow_state, (("circ", 2),), 1, True)


def local(coefficients, local_step, jacobian, harmonic_numbers, nodal_diameter):
    layers = coefficients.shape[2]
    cycle_size = lax.axis_size("circ")
    passages_all = PASS_DEV * cycle_size
    first_pass = lax.axis_index("circ") * PASS_DEV
    extra = 0
    owned = (first_pass - extra // 2 + jnp.arange(PASS_DEV + extra, dtype=jnp.int32)) % passages_all
    phases = phase_table(harmonic_numbers, nodal_diameter, owned, passages_all)
    fields = jnp.einsum(
        "pi,ivsc->pvsc",
        phases,
        lax.all_gather(coefficients, "circ", axis=3, tiled=True),
        precision=lax.Precision.HIGHEST,
    )
    fields = fields.reshape(PASS_DEV + extra, VARS, layers, PITCH, AXIAL)
    flow_state = fields.transpose(1, 2, 0, 3, 4).reshape(VARS, layers, PASS_DEV * PITCH, AXIAL)
    pitch_pad = send_rims(flow_state)
    span_pad = extended(flow_state, (("span", 1),), 1, False)
    return section_update(flow_state, span_pad, pitch_pad, jacobian, local_step)


def solution(mesh):
    in_specs = (P(None, None, "span", "circ"), P("span", "circ", None), P(), P(), P())
    out_specs = P(None, "span", "circ", None)
    return jax.shard_map(local, mesh=mesh, in_specs=in_specs, out_specs=out_specs, check_vma=False)
```

profile of v0, /device:TPU:1, one launch (start us, length us, event | category | flops | bytes accessed | tf_op | source)
XLA Modules:
  0.0 546.3 jit_solution(13596435359046372487)
XLA Ops:
  6.5 0.0 all-gather.2.cloned.1.call-start
  6.5 0.7 all-gather.2.cloned.1.call-update
  7.9 0.7 and_select_fusion.2
  8.6 0.1 fusion.29
  8.7 0.8 fusion.39
  9.5 0.9 broadcast_multiply_fusion
  10.5 465.5 %all-gather.2.cloned.1.call-done = f32[65,5,4,4096]{0,3,2,1:T(8,128)} async-done(((f32[65,5,4,64]{0,3,2,1:T(8,128)}), f32[65,5,4,4096]{0,3,2,1:T(8,128)}) %all-gather.2.cloned.1.call-update) | async-done | bytes 21299216 | tf_op jit(solution)/shard_map/all_gather | solution.py:71
  476.0 38.7 %fusion.21 = f32[2,5,4,4096]{3,0,2,1:T(2,128)S(1)} fusion(f32[65,5,4,4096]{0,3,2,1:T(8,128)} %all-gather.2.cloned.1.call-done, f32[2,32]{1,0:T(2,128)S(1)} %get-tuple-element.13, f32[2,32]{1,0:T(2,128)S(1)} %get-tuple-element.12, f32[65]{0:T(128)S(1)} %pad.13.clone), kind=kOutput, calls=%fused_computation.46 | convolution fusion | flops 127795456 | bytes 21955332 | tf_op jit(solution)/shard_map/pi,ivsc->pvsc/dot_general | solution.py:68
  514.7 0.6 reshape.31
  515.3 0.4 copy.6
  515.8 0.1 collective-permute-start.3
  515.9 5.7 %collective-permute-start.2 = (f32[5,4,1,256]{3,0,2,1:T(8,128)S(1)}, f32[5,4,1,256]{3,0,2,1:T(8,128)S(1)}, u32[]{:S(2)}, u32[]{:S(2)}) collective-permute-start(f32[5,4,1,256]{3,0,2,1:T(8,128)S(1)} %get-tuple-element.8), channel_id=1, source_target_pairs={{4,0},{8,4},{12,8},{16,12},{20,16},{24,20},{28,24},{32,28},{36,32}... | collective-permute-start | bytes 61448 | tf_op jit(solution)/shard_map/ppermute | solution.py:23
  521.5 5.6 %collective-permute-start.1 = (f32[5,1,32,256]{3,0,2,1:T(8,128)S(1)}, f32[5,1,32,256]{3,0,2,1:T(8,128)S(1)}, u32[]{:S(2)}, u32[]{:S(2)}) collective-permute-start(f32[5,1,32,256]{3,0,2,1:T(8,128)S(1)} %get-tuple-element.5), channel_id=1, source_target_pairs={{0,1},{1,2},{2,3},{4,5},{5,6},{6,7},{8,9},{9,10},{10,11},{12,13},{... | collective-permute-start | bytes 491528 | tf_op jit(solution)/shard_map/ppermute | solution.py:22
  527.1 2.1 collective-permute-start
  529.2 1.4 convolution_bitcast_fusion
  530.7 0.0 collective-permute-done.3
  530.7 0.0 collective-permute-done.2
  530.7 1.1 convolution_bitcast_fusion.1
  531.8 0.0 collective-permute-done.1
  531.8 4.5 collective-permute-done
  536.3 2.0 fusion.6
  538.4 1.0 copy.10
  (4 shorter events, 0.1 us)
Async XLA Ops:
  6.5 469.5 %all-gather.2.cloned.1.call-start = ((), (), s32[]{:S(2)}) async-start(), calls=%async_computation | async-start | bytes 42598400 | tf_op jit(solution)/shard_map/all_gather | solution.py:71
  515.8 14.9 %collective-permute-start.3 = (f32[5,4,1,256]{3,0,2,1:T(8,128)S(1)}, f32[5,4,1,256]{3,0,2,1:T(8,128)S(1)}, u32[]{:S(2)}, u32[]{:S(2)}) collective-permute-start(f32[5,4,1,256]{3,0,2,1:T(8,128)S(1)} %get-tuple-element.7), channel_id=1, source_target_pairs={{0,4},{4,8},{8,12},{12,16},{16,20},{20,24},{24,28},{28,32},{32,36}... | collective-permute-start | bytes 61448 | tf_op jit(solution)/shard_map/ppermute | solution.py:22
  515.9 14.8 %collective-permute-start.2 = (f32[5,4,1,256]{3,0,2,1:T(8,128)S(1)}, f32[5,4,1,256]{3,0,2,1:T(8,128)S(1)}, u32[]{:S(2)}, u32[]{:S(2)}) collective-permute-start(f32[5,4,1,256]{3,0,2,1:T(8,128)S(1)} %get-tuple-element.8), channel_id=1, source_target_pairs={{4,0},{8,4},{12,8},{16,12},{20,16},{24,20},{28,24},{32,28},{36,32}... | collective-permute-start | bytes 61448 | tf_op jit(solution)/shard_map/ppermute | solution.py:23
  521.5 10.3 %collective-permute-start.1 = (f32[5,1,32,256]{3,0,2,1:T(8,128)S(1)}, f32[5,1,32,256]{3,0,2,1:T(8,128)S(1)}, u32[]{:S(2)}, u32[]{:S(2)}) collective-permute-start(f32[5,1,32,256]{3,0,2,1:T(8,128)S(1)} %get-tuple-element.5), channel_id=1, source_target_pairs={{0,1},{1,2},{2,3},{4,5},{5,6},{6,7},{8,9},{9,10},{10,11},{12,13},{... | collective-permute-start | bytes 491528 | tf_op jit(solution)/shard_map/ppermute | solution.py:22
  527.1 9.2 %collective-permute-start = (f32[5,1,32,256]{3,0,2,1:T(8,128)S(1)}, f32[5,1,32,256]{3,0,2,1:T(8,128)S(1)}, u32[]{:S(2)}, u32[]{:S(2)}) collective-permute-start(f32[5,1,32,256]{3,0,2,1:T(8,128)S(1)} %get-tuple-element.6), channel_id=1, source_target_pairs={{1,0},{2,1},{3,2},{5,4},{6,5},{7,6},{9,8},{10,9},{11,10},{13,12},{... | collective-permute-start | bytes 491528 | tf_op jit(solution)/shard_map/ppermute | solution.py:23
Sparse Core Ops, SparseCore 0:
  9.1 466.8 all-gather.1
where the time goes:
time: 547 us; the launch traced here: 546 us
  waiting for transfers between devices  471 us (86%)
  matrix products  43.3 us (8%)
  between operations  14.2 us (3%)
  starting transfers between devices  13.4 us (2%)
    all_gather x1, waiting for transfers between devices, local(): lax.all_gather(coefficients, 'circ', axis=3, tiled=True)  466 us
    dot_general x1, matrix products, local(): jnp.einsum('pi,ivsc->pvsc', phases, lax.all_gather(coefficients, 'circ',...  38.7 us
  transfers between devices with their start and end apart: 5, of which 2 were waited for; matrix products, arithmetic and copies ran while one was open for 1% of the time, Pallas kernels for 0%

commit v1 on v0

--- a/solution.py
+++ b/solution.py
@@ -68,7 +68,9 @@
     fields = jnp.einsum(
         "pi,ivsc->pvsc",
         phases,
-        lax.all_gather(coefficients, "circ", axis=3, tiled=True),
+        jnp.concatenate(
+            lax.all_to_all(jnp.stack([coefficients] * lax.axis_size("circ")), "circ", 0, 0), axis=3
+        ),
         precision=lax.Precision.HIGHEST,
     )
     fields = fields.reshape(PASS_DEV + extra, VARS, layers, PITCH, AXIAL)

time: 547 us -> 1240 us (2.27)
  the two profiles are of different devices: /device:TPU:1 before, /device:TPU:60 now
where the time goes in v1:
time: 1240 us
  waiting for transfers between devices  1060 us (85%)
  local copies, waits for them, and re-layouts  123 us (10%)
  matrix products  33.8 us (3%)
  starting transfers between devices  19 us (2%)
    all_to_all x1, waiting for transfers between devices, local(): lax.all_to_all(jnp.stack([coefficients] * lax.axis_size('circ')), 'circ',...  1060 us
    reshape x2, local copies, waits for them, and re-layouts, local(): jnp.concatenate(lax.all_to_all(jnp.stack([coefficients] * lax.axis_size('...  81.5 us
    dot_general x1, matrix products, local(): jnp.einsum('pi,ivsc->pvsc', phases, jnp.concatenate(lax.all_to_all(jnp.st...  29.2 us
    dot_general x1, local copies, waits for them, and re-layouts, local(): jnp.einsum('pi,ivsc->pvsc', phases, jnp.concatenate(lax.all_to_all(jnp.st...  25.7 us
  transfers between devices with their start and end apart: 5, of which 3 were waited for; matrix products, arithmetic and copies ran while one was open for 0% of the time, Pallas kernels for 0%

profile of v1, /device:TPU:60, one launch (start us, length us, event | category | flops | bytes accessed | tf_op | source)
XLA Modules:
  0.0 1241.5 jit_solution(4097348490797647856)
XLA Ops:
  0.0 14.8 %stack.2 = f32[64,65,5,4,64]{1,4,3,2,0:T(8,128)} broadcast(f32[65,5,4,64]{0,3,2,1:T(8,128)} %param.5), dimensions={1,2,3,4} | broadcast | bytes 21632000 | tf_op jit(solution)/shard_map/stack | solution.py:72
  14.8 0.0 copy-start.2
  14.8 0.0 copy-start.1
  14.8 0.0 copy-start
  14.8 12.4 all-to-all-start
  27.9 0.0 copy-done.2
  27.9 0.1 fusion.33
  28.0 0.0 copy-done.1
  28.0 0.0 copy-done
  28.1 1058.6 %all-to-all-done = f32[64,65,5,4,64]{1,4,3,2,0:T(8,128)} async-done(((f32[64,65,5,4,64]{1,4,3,2,0:T(8,128)}), f32[64,65,5,4,64]{1,4,3,2,0:T(8,128)}, u32[]{:S(2)}, u32[]{:S(2)}) %all-to-all-start) | async-done | bytes 21299232 | tf_op jit(solution)/shard_map/all_to_all | solution.py:72
  1086.7 45.6 %copy.30 = f32[65,5,4,64,64]{4,3,2,1,0:T(8,128)} copy(f32[65,5,4,64,64]{0,4,2,1,3:T(8,128)} %bitcast.3) | data formatting | bytes 42598400 | tf_op jit(solution)/shard_map/reshape | solution.py:71
  1132.3 35.9 %reshape.39 = f32[65,5,4,4096]{3,2,1,0:T(4,128)} reshape(f32[65,5,4,64,64]{4,3,2,1,0:T(8,128)} %copy.30) | data formatting | bytes 42598400 | tf_op jit(solution)/shard_map/reshape | solution.py:71
  1168.2 25.7 %reshape.45 = f32[5,4,16,256,65]{3,2,1,0,4:T(8,128)} reshape(f32[5,4,4096,65]{2,1,0,3:T(4,128)} %bitcast.69) | data formatting | bytes 42598400 | tf_op jit(solution)/shard_map/pi,ivsc->pvsc/dot_general | solution.py:68
  1193.9 29.2 %fusion.9 = f32[5,4,2,16,256]{4,2,3,1,0:T(2,128)S(1)} fusion(f32[5,4,16,256,65]{3,2,1,0,4:T(8,128)} %reshape.45, f32[2,32]{1,0:T(2,128)S(1)} %get-tuple-element.13, f32[2,32]{1,0:T(2,128)S(1)} %get-tuple-element.12, f32[65]{0:T(128)S(1)} %pad.13.clone), kind=kOutput, calls=%fused_computation.14 | convolution fusion | flops 127795456 | bytes 21955332 | tf_op jit(solution)/shard_map/pi,ivsc->pvsc/dot_general | solution.py:68
  1223.1 0.4 copy.55
  1223.6 1.4 convolution_bitcast_fusion
  1225.0 0.3 collective-permute-start.2
  1225.3 2.0 collective-permute-start.3
  1227.3 1.9 collective-permute-start
  1229.2 2.4 collective-permute-start.1
  1231.7 0.0 collective-permute-done.2
  1231.7 0.0 collective-permute-done.3
  1231.7 1.1 convolution_bitcast_fusion.1
  1232.8 0.3 collective-permute-done
  1233.1 5.3 collective-permute-done.1
  1238.4 2.0 fusion.8
  1240.5 1.0 copy.48
  (7 shorter events, 0.1 us)
Async XLA Ops:
  14.8 13.1 %copy-start.2 = (s32[32]{0:T(128)S(1)}, s32[32]{0:T(128)}, u32[]{:S(2)}) copy-start(s32[32]{0:T(128)} %param.8) | copy-start | bytes 388
  14.8 13.3 %copy-start.1 = (f32[3,5,5]{2,0,1:T(4,128)S(1)}, f32[3,5,5]{2,0,1:T(4,128)}, u32[]{:S(2)}) copy-start(f32[3,5,5]{2,0,1:T(4,128)} %param.7) | copy-start | bytes 904
  14.8 13.3 %copy-start = (f32[4,32,256]{2,1,0:T(8,128)S(1)}, f32[4,32,256]{2,1,0:T(8,128)}, u32[]{:S(2)}) copy-start(f32[4,32,256]{2,1,0:T(8,128)} %param.6) | copy-start | bytes 393220
  14.8 1071.9 %all-to-all-start = ((f32[64,65,5,4,64]{1,4,3,2,0:T(8,128)}), f32[64,65,5,4,64]{1,4,3,2,0:T(8,128)}, u32[]{:S(2)}, u32[]{:S(2)}) async-start(f32[64,65,5,4,64]{1,4,3,2,0:T(8,128)} %stack.2), calls=%async_computation | async-start | bytes 83886080 | tf_op jit(solution)/shard_map/all_to_all | solution.py:72
  1225.0 6.7 collective-permute-start.2
  1225.3 6.4 collective-permute-start.3
  1227.3 5.8 collective-permute-start
  1229.2 9.2 collective-permute-start.1
